TPU v7x, 256 devices: a whole 4x4x8 slice. The times are simulated.
256 devices in a mesh: node: 32 (over z, x_lo, core), term: 8 (over x_hi, y).
Axes of the slice: x: 4 (x_hi: 2, x_lo: 2; x = x_hi * 2 + x_lo), y: 4, z: 8, core: 2. Of those that a mesh axis runs over, the one named last changes fastest.
Arguments:
- node_tensors: bfloat16 [32, 64, 4096], P('node'), may hold values from -0.046875 to 1.046875
- prim_ops: bfloat16 [32, 32, 2, 64, 64], P('node', 'term'), may hold values from -3.8 to 3.8, as said below
- active: int32 [32, 32, 2], P('node', 'term'), may hold values 0 or 1
- top_field: bfloat16 [32, 64, 64], P('term'), may hold values from -0.95 to 0.95, as said below
- node_map: int32 [32], replicated, may hold values from 0 to 31, as said below
Outputs:
- derivative: bfloat16 [32, 64, 4096], P('node', 'term')
Inputs may be any that keep to these rules, and one draw needn't show every extreme that they name: node_map holds every position 0 to 31 once; position 31 is no node; the slot of position 1 is the slot of position 0 plus 32 // 2, counted round. `prim_ops`: each operator is symmetric. `top_field`: each matrix is symmetric.
All inputs are finite; a program needn't handle non-finite values. No bound on the sum of `active` on one device may be relied on, other than what follows from the above.
Results may differ from a plain program's by a relative error of at most 0.025.
The roundings to bfloat16 on the way count: a program that leaves them out, or rounds other values in their place, can miss the bound.
Values may be sent and summed in bfloat16 or wider, within the bound.
A program may use at most 64 MiB of HBM per device.

v0:
```python
import jax
import jax.numpy as jnp
from jax import lax
from jax.sharding import PartitionSpec as P


def mode_one(matrix, tensor):
    extent = tensor.shape[0]
    return jnp.dot(matrix, tensor.reshape(extent, -1), preferred_element_type=jnp.float32).reshape(
        tensor.shape
    )


def mode_two(matrix, tensor):
    return jnp.einsum("ij,ajc->aic", matrix, tensor, preferred_element_type=jnp.float32)


def mode_three(matrix, tensor):
    extent = tensor.shape[2]
    return jnp.dot(
        tensor.reshape(-1, extent), matrix.T, preferred_element_type=jnp.float32
    ).reshape(tensor.shape)


def up_term(tensor, left_term, right_term):
    extent = tensor.shape[2]
    partial_one = mode_two(right_term, tensor).astype(jnp.bfloat16)
    weighted = mode_one(left_term, partial_one).astype(jnp.bfloat16)
    return jnp.dot(
        tensor.reshape(-1, extent).T,
        weighted.reshape(-1, extent),
        preferred_element_type=jnp.float32,
    ).astype(jnp.bfloat16)


def down_term(tensor, left_term, right_term, field_now):
    extent = tensor.shape[0]
    reduced = mode_three(field_now, tensor).astype(jnp.bfloat16)
    side_left = mode_two(right_term, reduced).astype(jnp.bfloat16)
    side_right = mode_one(left_term, reduced).astype(jnp.bfloat16)
    field_left = jnp.dot(
        tensor.reshape(extent, -1),
        side_left.reshape(extent, -1).T,
        preferred_element_type=jnp.float32,
    ).astype(jnp.bfloat16)
    field_right = jnp.einsum(
        "abc,adc->bd", tensor, side_right, preferred_element_type=jnp.float32
    ).astype(jnp.bfloat16)
    deriv_term = mode_one(left_term, side_left)
    return (field_left, field_right, deriv_term)


def per_device(node_tensors, prim_ops, active, top_field, node_map):
    nodes_axis = lax.axis_size("node")
    depths = nodes_axis.bit_length() - 1
    my_index = lax.axis_index("node")
    position = node_map[my_index]
    slot_ids = jnp.arange(nodes_axis, dtype=jnp.int32)

    def slot_of(target):
        return jnp.sum(jnp.where(node_map == target, slot_ids, 0))

    my_depth = jnp.zeros((), jnp.int32)
    for power in range(1, depths):
        my_depth = my_depth + jnp.where(position + 1 >= 2**power, 1, 0)
    my_depth = jnp.where(position >= nodes_axis - 1, -1, my_depth)
    left_slot = slot_of(2 * position + 1)
    right_slot = slot_of(2 * position + 2)
    parent_slot = slot_of((position - 1) // 2)
    from_left = position % 2 == 1
    extent = node_tensors.shape[1]
    tensor_here = node_tensors[0].reshape(extent, extent, extent)
    identity = jnp.eye(extent, dtype=jnp.bfloat16)
    leaf_terms = jnp.where(active[0][..., None, None] == 1, prim_ops[0], identity)

    def up_all(left_terms, right_terms):
        return lax.map(
            lambda pair: up_term(tensor_here, pair[0], pair[1]), (left_terms, right_terms)
        )

    number = leaf_terms.shape[0]
    left_terms = leaf_terms[:, 0]
    right_terms = leaf_terms[:, 1]
    empty = jnp.zeros((number, extent, extent), jnp.bfloat16)
    mine = lax.cond(my_depth == depths - 1, lambda: up_all(left_terms, right_terms), lambda: empty)
    for depth in range(depths - 2, -1, -1):
        gathered = lax.all_gather(mine[None], "node", axis=0, tiled=True)
        active_now = my_depth == depth
        left_terms = jnp.where(active_now, gathered[left_slot], left_terms)
        right_terms = jnp.where(active_now, gathered[right_slot], right_terms)
        if depth >= 1:
            mine = lax.cond(active_now, lambda: up_all(left_terms, right_terms), lambda: mine)
    field_here = top_field
    partial_value = jnp.zeros((extent, extent, extent), jnp.float32)
    for depth in range(depths):
        active_now = my_depth == depth

        def down_all():

            def step_term(total, items):
                field_left, field_right, deriv_term = down_term(
                    tensor_here, items[0], items[1], items[2]
                )
                return (total + deriv_term, (field_left, field_right))

            total, (lefts_all, rights_all) = lax.scan(
                step_term, partial_value, (left_terms, right_terms, field_here)
            )
            return (lefts_all, rights_all, total)

        field_left, field_right, partial_value = lax.cond(
            active_now, down_all, lambda: (empty, empty, partial_value)
        )
        if depth < depths - 1:
            both_sides = jnp.stack([field_left, field_right], axis=1)
            gathered = lax.all_gather(both_sides[None], "node", axis=0, tiled=True)
            from_parent = gathered[parent_slot]
            arrived = jnp.where(from_left, from_parent[:, 0], from_parent[:, 1])
            field_here = jnp.where(my_depth == depth + 1, arrived, field_here)
    summed = lax.psum_scatter(
        partial_value.astype(jnp.bfloat16), "term", scatter_dimension=0, tiled=True
    ).astype(jnp.float32)
    return summed.astype(jnp.bfloat16).reshape(summed.shape[0], extent * extent)[None]


def solution(mesh):
    placed = (
        P("node", None, None),
        P("node", "term", None, None, None),
        P("node", "term", None),
        P("term", None, None),
        P(),
    )
    return jax.shard_map(
        per_device, mesh=mesh, in_specs=placed, out_specs=P("node", "term", None), check_vma=False
    )
```

profile of v0, /device:TPU:24, one launch (start us, length us, event | category | flops | bytes accessed | tf_op | source)
XLA Modules:
  0.0 1176.5 jit_solution(16916686037055861873)
XLA Ops:
  9.3 2.1 reshape_squeeze.3
  20.9 101.2 %all-gather.17.cloned.1.call-done = bf16[128,64,64]{2,1,0:T(8,128)(2,1)} async-done(((bf16[4,64,64]{2,1,0:T(8,128)(2,1)}), bf16[128,64,64]{2,1,0:T(8,128)(2,1)}) %all-gather.17.cloned.1.call-update) | async-done | bytes 1048592 | tf_op jit(solution)/shard_map/all_gather | solution.py:87
  123.0 40.1 %conditional.10 = (bf16[4,64,64]{1,2,0:T(8,128)(2,1)}) conditional(s32[]{:T(128)} %convert_element_type.243, bf16[4,64,64]{1,2,0:T(8,128)(2,1)} %get-tuple-element.1470, (bf16[4,64,64]{2,1,0:T(8,128)(2,1)S(1)}, bf16[4,64,64]{2,1,0:T(8,128)(2,1)S(1)}, bf16[64,64,64]{2,1,0:T(8,128)(2,1)S(1)}, bf16[1,64,4096]{2,1,0:T(8,128)(2,1)S(1)}) %tuple.289), branch_computations={%region_6.7_spmd, %region_7.10_spmd} | conditional | flops 101191680 | bytes 9487005 | solution.py:92
  123.0 40.1 %while.105 = (s32[]{:T(128)}, bf16[4,64,64]{1,2,0:T(8,128)(2,1)}, bf16[4,64,64]{2,1,0:T(8,128)(2,1)S(1)}, bf16[4,64,64]{2,1,0:T(8,128)(2,1)S(1)}, bf16[64,64,64]...) while((s32[]{:T(128)}, bf16[4,64,64]{1,2,0:T(8,128)(2,1)}, ...), condition=%wide.region_9.9_spmd, body=%wide.region_8.8_spmd.sunk | while | flops 101191680 | bytes 9486933 | solution.py:77
  124.7 2.1 convolution_convert_fusion.44
  126.8 3.3 copy.279
  134.7 2.1 convolution_convert_fusion.44
  136.8 3.3 copy.279
  144.7 2.1 convolution_convert_fusion.44
  146.9 3.3 copy.279
  154.8 2.1 convolution_convert_fusion.44
  156.9 3.3 copy.279
  164.7 63.6 %all-gather.19.cloned.1.call-done = bf16[128,64,64]{2,1,0:T(8,128)(2,1)} async-done(((bf16[4,64,64]{2,1,0:T(8,128)(2,1)}), bf16[128,64,64]{2,1,0:T(8,128)(2,1)}) %all-gather.19.cloned.1.call-update) | async-done | bytes 1048592 | tf_op jit(solution)/shard_map/all_gather | solution.py:87
  231.0 101.9 %all-gather.21.cloned.1.call-done = bf16[128,64,64]{2,1,0:T(8,128)(2,1)} async-done(((bf16[4,64,64]{2,1,0:T(8,128)(2,1)}), bf16[128,64,64]{2,1,0:T(8,128)(2,1)}) %all-gather.21.cloned.1.call-update) | async-done | bytes 1048592 | tf_op jit(solution)/shard_map/all_gather | solution.py:87
  333.8 1.6 copy.164
  335.5 100.8 %all-gather.23.cloned.1.call-done = bf16[128,64,64]{2,1,0:T(8,128)(2,1)} async-done(((bf16[4,64,64]{2,1,0:T(8,128)(2,1)}), bf16[128,64,64]{2,1,0:T(8,128)(2,1)}) %all-gather.23.cloned.1.call-update) | async-done | bytes 1048592 | tf_op jit(solution)/shard_map/all_gather | solution.py:87
  437.2 3.3 conditional.13
  437.2 1.6 broadcast_in_dim.64
  440.5 1.5 pad_maximum_fusion
  446.2 144.8 %all-gather.25.cloned.1.call-done = bf16[128,2,64,64]{2,3,0,1:T(8,128)(2,1)} async-done(((bf16[4,2,64,64]{2,3,0,1:T(8,128)(2,1)}), bf16[128,2,64,64]{2,3,0,1:T(8,128)(2,1)}) %all-gather.25.cloned.1.call-update) | async-done | bytes 2097168 | tf_op jit(solution)/shard_map/all_gather | solution.py:116
  595.1 149.1 %all-gather.27.cloned.1.call-done = bf16[128,2,64,64]{2,3,0,1:T(8,128)(2,1)} async-done(((bf16[4,2,64,64]{2,3,0,1:T(8,128)(2,1)}), bf16[128,2,64,64]{2,3,0,1:T(8,128)(2,1)}) %all-gather.27.cloned.1.call-update) | async-done | bytes 2097168 | tf_op jit(solution)/shard_map/all_gather | solution.py:116
  748.4 150.3 %all-gather.29.cloned.1.call-done = bf16[128,2,64,64]{2,3,0,1:T(8,128)(2,1)} async-done(((bf16[4,2,64,64]{2,3,0,1:T(8,128)(2,1)}), bf16[128,2,64,64]{2,3,0,1:T(8,128)(2,1)}) %all-gather.29.cloned.1.call-update) | async-done | bytes 2097168 | tf_op jit(solution)/shard_map/all_gather | solution.py:116
  899.9 83.3 %conditional.16 = (f32[64,64,64]{2,0,1:T(8,128)}, bf16[4,1,64,64]{3,2,1,0:T(8,128)(2,1)S(1)}, bf16[4,1,64,64]{3,2,1,0:T(8,128)(2,1)S(1)}) conditional(s32[]{:T(128)} %convert_element_type.243, f32[64,64,64]{2,0,1:T(8,128)} %get-tuple-element.603, (bf16[4,64,64]{2,1,0:T(8,128)(2,1)S(1)}, bf16[4,64,64]{2,1,0:T(8,128)(2,1)S(1)}, ...), branch_computations={%region_31.32_spmd, %region_32.35_spmd} | conditional | flops 202383360 | bytes 18579692 | solution.py:111
  900.1 82.8 %while.110 = (s32[]{:T(128)}, f32[64,64,64]{2,0,1:T(8,128)}, bf16[4,64,64]{1,2,0:T(8,128)(2,1)S(1)}, bf16[4,64,64]{1,2,0:T(8,128)(2,1)S(1)}, bf16[4,64,64]{2,1,0...) while((s32[]{:T(128)}, f32[64,64,64]{2,0,1:T(8,128)}, ...), condition=%wide.region_34.34_spmd, body=%wide.region_33.33_spmd.sunk | while | flops 202383360 | bytes 18448508 | solution.py:106
  901.8 2.1 convert_element_type.422
  903.9 2.0 fusion.312
  907.2 2.1 reshape.156
  910.6 4.4 convolution_add_fusion.9
  915.8 1.6 convert_element_type.423
  922.5 2.1 convert_element_type.422
  924.6 2.0 fusion.312
  928.0 2.1 reshape.156
  931.4 4.4 convolution_add_fusion.9
  936.5 1.6 convert_element_type.423
  943.2 2.1 convert_element_type.422
  945.3 2.0 fusion.312
  948.7 2.1 reshape.156
  952.1 4.4 convolution_add_fusion.9
  957.3 1.6 convert_element_type.423
  963.9 2.1 convert_element_type.422
  966.0 2.0 fusion.312
  969.4 2.1 reshape.156
  972.8 4.4 convolution_add_fusion.9
  978.0 1.6 convert_element_type.423
  984.0 65.9 %all-gather.31.cloned.1.call-done = bf16[128,2,64,64]{3,2,1,0:T(8,128)(2,1)} async-done(((bf16[4,2,64,64]{3,2,1,0:T(8,128)(2,1)}), bf16[128,2,64,64]{3,2,1,0:T(8,128)(2,1)}) %all-gather.31.cloned.1.call-update) | async-done | bytes 2097168 | tf_op jit(solution)/shard_map/all_gather | solution.py:116
  1050.1 1.8 convert_element_type.248
  1052.6 1.6 reshape.139
  1054.2 115.2 %reduce-scatter.4.cloned.1.call-done = bf16[8,4096]{1,0:T(8,128)(2,1)} async-done(((bf16[64,4096]{1,0:T(8,128)(2,1)}), bf16[8,4096]{1,0:T(8,128)(2,1)}) %reduce-scatter.4.cloned.1.call-update) | async-done | bytes 65552
  (128 shorter events, 80.7 us)
Async XLA Ops:
  6.5 6.6 copy-start
  6.5 115.5 %all-gather.17.cloned.1.call-start = ((), (), s32[]{:S(2)}) async-start(), calls=%async_computation.1 | async-start | bytes 2162688 | tf_op jit(solution)/shard_map/all_gather | solution.py:87
  13.1 3.7 copy-start.2
  15.3 212.9 %all-gather.19.cloned.1.call-start = ((), (), s32[]{:S(2)}) async-start(), calls=%async_computation.2 | async-start | bytes 2162688 | tf_op jit(solution)/shard_map/all_gather | solution.py:87
  164.6 168.3 %all-gather.21.cloned.1.call-start = ((), (), s32[]{:S(2)}) async-start(), calls=%async_computation.3 | async-start | bytes 2162688 | tf_op jit(solution)/shard_map/all_gather | solution.py:87
  231.0 205.3 %all-gather.23.cloned.1.call-start = ((), (), s32[]{:S(2)}) async-start(), calls=%async_computation.4 | async-start | bytes 2162688 | tf_op jit(solution)/shard_map/all_gather | solution.py:87
  333.8 103.4 %copy-start.1 = (bf16[4,64,64]{2,1,0:T(8,128)(2,1)S(1)}, bf16[4,64,64]{2,1,0:T(8,128)(2,1)}, u32[]{:S(2)}) copy-start(bf16[4,64,64]{2,1,0:T(8,128)(2,1)} %param.44) | copy-start | bytes 98308
  335.4 255.5 %all-gather.25.cloned.1.call-start = ((), (), s32[]{:S(2)}) async-start(), calls=%async_computation.5 | async-start | bytes 4325376 | tf_op jit(solution)/shard_map/all_gather | solution.py:116
  442.1 302.2 %all-gather.27.cloned.1.call-start = ((), (), s32[]{:S(2)}) async-start(), calls=%async_computation.6 | async-start | bytes 4325376 | tf_op jit(solution)/shard_map/all_gather | solution.py:116
  595.1 303.7 %all-gather.29.cloned.1.call-start = ((), (), s32[]{:S(2)}) async-start(), calls=%async_computation.7 | async-start | bytes 4325376 | tf_op jit(solution)/shard_map/all_gather | solution.py:116
  748.4 301.4 %all-gather.31.cloned.1.call-start = ((), (), s32[]{:S(2)}) async-start(), calls=%async_computation.8 | async-start | bytes 4325376 | tf_op jit(solution)/shard_map/all_gather | solution.py:116
  983.9 185.6 %reduce-scatter.4.cloned.1.call-start = ((), (), s32[]{:S(2)}) async-start(), calls=%async_computation.9 | async-start | bytes 589824
Sparse Core Ops, SparseCore 0:
  15.5 106.5 all-gather.16
  164.8 63.4 all-gather.18
  231.1 101.7 all-gather.20
  335.6 100.6 all-gather.22
  442.2 148.7 all-gather.24
  595.2 149.0 all-gather.26
  748.5 150.2 all-gather.28
  984.0 65.7 all-gather.30
  1054.4 115.0 reduce-scatter.3
where the time goes:
time: 1190 us; the launch traced here: 1180 us
  waiting for transfers between devices  993 us (83%)
  local copies, waits for them, and re-layouts  93.7 us (8%)
  matrix products  50.1 us (4%)
  between operations  24.2 us (2%)
  other arithmetic  13.1 us (1%)
    all_gather x4, waiting for transfers between devices, per_device(): gathered = lax.all_gather(both_sides[None], 'node', axis=0, tiled=True)  510 us
    all_gather x4, waiting for transfers between devices, per_device(): gathered = lax.all_gather(mine[None], 'node', axis=0, tiled=True)  367 us
    unnamed x10, waiting for transfers between devices  115 us
    dot_general x12, matrix products, mode_one(): jnp.dot(matrix, tensor.reshape(extent, -1), preferred_element_type=jnp.fl...  30.6 us
  transfers between devices with their start and end apart: 9, of which 9 were waited for; matrix products, arithmetic and copies ran while one was open for 0% of the time, Pallas kernels for 0%

commit v1 on v0

v1 whole, which is shorter than its diff:
```python
import functools

import jax
import jax.numpy as jnp
from jax import lax
from jax.experimental import pallas as pl
from jax.experimental.pallas import tpu as pltpu
from jax.sharding import PartitionSpec as P

MESH = pl.DeviceIdType.MESH
F32 = jnp.float32
BF16 = jnp.bfloat16
LEVELS = 4


def mm(x, y):
    return lax.dot_general(x, y, (((1,), (0,)), ((), ())), preferred_element_type=F32)


def mm_nt(x, y):
    return lax.dot_general(x, y, (((1,), (1,)), ((), ())), preferred_element_type=F32)


def iota(shape, dim):
    return lax.broadcasted_iota(jnp.int32, shape, dim)


def kernel(
    n_term,
    tbl,
    a1,
    a1p,
    a3,
    an2,
    an2p,
    leaf,
    top,
    out,
    e_r,
    e_l,
    j_r,
    j_l,
    m_r,
    m_l,
    m_m,
    perm,
    x_buf,
    y_buf,
    w_buf,
    ra_buf,
    la_buf,
    v_buf,
    bd_buf,
    lr_buf,
    m_buf,
    pieces,
    rs,
    *rest,
):
    zbuf = rest[0:4]
    psend = rest[4:8]
    prbuf = rest[8:12]
    dpl = rest[12:16]
    zsend = rest[16:20]
    zr = rest[20:24]
    us, ur, ps, pr, ds_, dr, zs, zr_sem, ts, tr = rest[24:34]

    node = lax.axis_index("node")
    term = lax.axis_index("term")
    z = node // 4
    j = lax.rem(node, 4)

    def at_node(zt, jt):
        return {"node": zt * 4 + jt}

    partners = []
    for dz in range(1, 8):
        partners.append(at_node(lax.rem(z + dz, 8), j))
    for dj in range(1, 4):
        partners.append(at_node(z, lax.rem(j + dj, 4)))
    for dt in range(1, n_term):
        partners.append({"term": lax.rem(term + dt, n_term)})
    barrier = pltpu.get_barrier_semaphore()
    for partner in partners:
        pl.semaphore_signal(barrier, inc=1, device_id=partner, device_id_type=MESH)

    rows, cols = iota((256, 64), 0), iota((256, 64), 1)
    by, bx = rows // 16, lax.rem(rows // 4, 4)
    e_r[...] = jnp.where(cols == bx * 16 + by, 1.0, 0.0).astype(BF16)
    e_l[...] = jnp.where(cols == lax.rem(rows, 64), 1.0, 0.0).astype(BF16)
    rows, cols = iota((128, 256), 0), iota((128, 256), 1)
    for half in range(2):
        k = rows - 64 * half
        j_r[half] = jnp.where(k == lax.rem(cols, 64), 1.0, 0.0).astype(BF16)
        j_l[half] = jnp.where(k == (cols // 16) * 4 + lax.rem(cols, 4), 1.0, 0.0).astype(BF16)
    rows, cols = iota((256, 256), 0), iota((256, 256), 1)
    m_r[...] = jnp.where(lax.rem(rows, 4) == cols // 64, 1.0, 0.0)
    same_bx = rows // 64 == lax.rem(cols // 4, 4)
    m_l[...] = jnp.where(same_bx, 1.0, 0.0)
    m_m[...] = jnp.where(rows // 64 == cols // 64, 1.0, 0.0)
    same_a = lax.rem(rows, 64) == (cols // 16) * 4 + lax.rem(cols, 4)
    perm[...] = jnp.where(same_bx & same_a, 1.0, 0.0).astype(BF16)
    low = iota((16, 128), 1) < 64
    low64 = iota((64, 128), 1) < 64

    def expand(pair, half, e, jm, mask):
        spread = mm(e[...], pair).astype(BF16)
        return (mm(spread, jm[half]) * mask[...]).astype(BF16)

    def op_on_mid(src, side, dst):
        def body(rp, _):
            pair = lr_buf[side, pl.ds(pl.multiple_of(rp * 64, 64), 64), :]
            for half in range(2):
                weight = expand(pair, half, e_r, j_r, m_r)
                r = rp * 2 + half
                for g in range(4):
                    o = mm(weight, src[:, g * 256 : (g + 1) * 256])
                    for k in range(2):
                        for i in range(8):
                            u = o[32 * i : 32 * i + 16, 128 * k : 128 * k + 128]
                            v = o[32 * i + 16 : 32 * i + 32, 128 * k : 128 * k + 128]
                            ur_, vr_ = pltpu.roll(u, 64, 1), pltpu.roll(v, 64, 1)
                            hi = (4 * g + 2 * k) * 16
                            lanes = slice(i * 128, i * 128 + 128)
                            dst[r, hi : hi + 16, lanes] = jnp.where(low, u, vr_).astype(BF16)
                            dst[r, hi + 16 : hi + 32, lanes] = jnp.where(low, ur_, v).astype(BF16)
            return 0

        lax.fori_loop(0, 2, body, 0)

    def up(send):
        op_on_mid(a1, 1, x_buf)

        def body(rp, _):
            span = pl.ds(pl.multiple_of(rp * 64, 64), 64)
            pair = lr_buf[0, span, :]
            both = []
            for half in range(2):
                weight = expand(pair, half, e_l, j_l, m_l)
                r = rp * 2 + half
                acc = jnp.zeros((256, 256), F32)
                for g in range(4):
                    w = mm(weight, x_buf[r, :, g * 256 : (g + 1) * 256]).astype(BF16)
                    acc = acc + mm(a3[g], w)
                s = jnp.where(low64, acc[0:64, 0:128], acc[64:128, 0:128]) + jnp.where(
                    low64, acc[128:192, 128:256], acc[192:256, 128:256]
                )
                both.append(s + pltpu.roll(s, 64, 1))
            send[z, span, :] = jnp.where(low64, both[0], both[1]).astype(BF16)
            return 0

        lax.fori_loop(0, 2, body, 0)

    def natural(src, dst):
        def body(r, _):
            for g in range(4):
                lanes = slice(g * 256, g * 256 + 256)
                dst[r, :, lanes] = mm(perm[...], src[r, :, lanes]).astype(BF16)
            return 0

        lax.fori_loop(0, 4, body, 0)

    def weighted():
        def body(rp, _):
            pair = lr_buf[0, pl.ds(pl.multiple_of(rp * 64, 64), 64), :]
            for half in range(2):
                weight = expand(pair, half, e_l, j_l, m_l)
                r = rp * 2 + half
                for g in range(4):
                    lanes = slice(g * 256, g * 256 + 256)
                    w_buf[r, :, lanes] = mm(weight, x_buf[r, :, lanes]).astype(BF16)
            return 0

        lax.fori_loop(0, 2, body, 0)

    def field():
        def body(rp, _):
            pair = m_buf[pl.ds(pl.multiple_of(rp * 64, 64), 64), :]
            for half in range(2):
                bd_buf[rp * 2 + half] = expand(pair, half, e_l, j_r, m_m)
            return 0

        lax.fori_loop(0, 2, body, 0)

    def down(src, base, dst, slot):
        def body(r, _):
            span = pl.ds(pl.multiple_of(r * 64, 64), 64)
            for g in range(4):
                lanes = slice(g * 256, g * 256 + 256)
                v = mm(src[r, :, lanes], bd_buf[r]).astype(BF16)
                for q in range(4):
                    v_buf[q, span, lanes] = v[q * 64 : q * 64 + 64]
            return 0

        lax.fori_loop(0, 4, body, 0)
        acc = jnp.zeros((256, 128), F32)
        for q in range(4):
            acc = acc + mm_nt(v_buf[q], base[:, q * 1024 : q * 1024 + 1024])
        for rp in range(2):
            dst[slot, rp * 64 : rp * 64 + 64, :] = jnp.where(
                low64, acc[rp * 128 : rp * 128 + 64], acc[rp * 128 + 64 : rp * 128 + 128]
            ).astype(BF16)

    pending = []
    for level in range(LEVELS):
        prbuf[level][4] = leaf[...]
    for level in range(LEVELS):
        zr[level][8] = top[...]

    lr_buf[...] = leaf[...]
    for level in range(LEVELS):
        zb, sb, rb = zbuf[level], psend[level], prbuf[level]
        up(zb)
        if level == 0:
            pl.semaphore_wait(barrier, len(partners))
        copies = []
        for dz in (4, 3, 5, 2, 6, 1, 7):
            copy = pltpu.make_async_remote_copy(
                src_ref=zb.at[z],
                dst_ref=zb.at[z],
                send_sem=us.at[level * 8 + dz],
                recv_sem=ur.at[level * 8 + dz],
                device_id=at_node(lax.rem(z + dz, 8), j),
                device_id_type=MESH,
            )
            copy.start()
            copies.append(copy)
        for copy in copies:
            copy.wait_recv()
        pending += copies
        copies = []
        for dj in (1, 2, 3, 0):
            if dj == 0:
                rb[j, 0] = zb[tbl[0]]
                rb[j, 1] = zb[tbl[1]]
                continue
            sb[dj, 0] = zb[tbl[2 * dj]]
            sb[dj, 1] = zb[tbl[2 * dj + 1]]
            copy = pltpu.make_async_remote_copy(
                src_ref=sb.at[dj],
                dst_ref=rb.at[j],
                send_sem=ps.at[level * 4 + dj],
                recv_sem=pr.at[level * 4 + dj],
                device_id=at_node(z, lax.rem(j + dj, 4)),
                device_id_type=MESH,
            )
            copy.start()
            copies.append(copy)
        for copy in copies:
            copy.wait_recv()
        pending += copies
        lr_buf[0] = rb[tbl[8], 0]
        lr_buf[1] = rb[tbl[9], 1]

    m_buf[...] = top[...]
    op_on_mid(a1, 1, x_buf)
    natural(x_buf, ra_buf)
    op_on_mid(a1p, 0, y_buf)
    natural(y_buf, la_buf)

    for level in range(LEVELS):
        db, sb, rb = dpl[level], zsend[level], zr[level]
        field()
        down(ra_buf, an2, db, 2 * j)
        down(la_buf, an2p, db, 2 * j + 1)
        copies = []
        for dj in (1, 2, 3):
            copy = pltpu.make_async_remote_copy(
                src_ref=db.at[pl.ds(2 * j, 2)],
                dst_ref=db.at[pl.ds(2 * j, 2)],
                send_sem=ds_.at[level * 4 + dj],
                recv_sem=dr.at[level * 4 + dj],
                device_id=at_node(z, lax.rem(j + dj, 4)),
                device_id_type=MESH,
            )
            copy.start()
            copies.append(copy)
        if level == 0:
            weighted()
        for copy in copies:
            copy.wait_recv()
        pending += copies
        copies = []
        for dz in (4, 3, 5, 2, 6, 1, 7, 0):
            if dz == 0:
                rb[z] = db[tbl[10]]
                continue
            sb[dz] = db[tbl[10 + dz]]
            copy = pltpu.make_async_remote_copy(
                src_ref=sb.at[dz],
                dst_ref=rb.at[z],
                send_sem=zs.at[level * 8 + dz],
                recv_sem=zr_sem.at[level * 8 + dz],
                device_id=at_node(lax.rem(z + dz, 8), j),
                device_id_type=MESH,
            )
            copy.start()
            copies.append(copy)
        for copy in copies:
            copy.wait_recv()
        pending += copies
        m_buf[...] = rb[tbl[18]]

    field()
    height = 64 // n_term

    def last(g, _):
        lanes = pl.ds(pl.multiple_of(g * 256, 256), 256)
        acc = jnp.zeros((256, 256), F32)
        for r in range(4):
            acc = acc + mm(w_buf[r, :, lanes], bd_buf[r])
        for q in range(4):
            span = pl.ds(pl.multiple_of(q * 1024 + g * 256, 256), 256)
            for t in range(n_term):
                first = q * 64 + t * height
                pieces[t, :, span] = acc[first : first + height].astype(BF16)
        return 0

    lax.fori_loop(0, 4, last, 0)
    copies = []
    for dt in range(1, n_term):
        target = lax.rem(term + dt, n_term)
        copy = pltpu.make_async_remote_copy(
            src_ref=pieces.at[target],
            dst_ref=rs.at[dt],
            send_sem=ts.at[dt],
            recv_sem=tr.at[dt],
            device_id={"term": target},
            device_id_type=MESH,
        )
        copy.start()
        copies.append(copy)
    total = pieces[term].astype(F32)
    for copy in copies:
        copy.wait_recv()
    for dt in range(1, n_term):
        total = total + rs[dt].astype(F32)
    out[...] = total.astype(BF16)
    pending += copies
    for copy in pending:
        copy.wait_send()


def pairs(mats):
    lead = mats.shape[:-3]
    x = mats.reshape(lead + (2, 2, 64, 64))
    return jnp.swapaxes(x, -3, -2).reshape(lead + (128, 128))


def per_device(n_term, node_tensors, prim_ops, active, top_field, node_map):
    node = lax.axis_index("node")
    z, j = node // 4, node % 4
    tensor = node_tensors[0].reshape(64, 64, 64)
    swapped = jnp.swapaxes(tensor, 0, 1)

    def split(x):
        return x.reshape(16, 4, 64, 64).transpose(1, 2, 0, 3).reshape(256, 1024)

    a1 = split(tensor)
    a1p = split(swapped)
    a3 = tensor.reshape(64, 4, 4, 4, 64).transpose(2, 3, 4, 1, 0).reshape(4, 256, 256)
    flat, flatp = tensor.reshape(64, 4096), swapped.reshape(64, 4096)
    an2 = jnp.concatenate([flat, flat], axis=0)
    an2p = jnp.concatenate([flatp, flatp], axis=0)
    identity = jnp.eye(64, dtype=BF16)
    leaf = jnp.where(active[0][..., None, None] == 1, prim_ops[0], identity)
    leaf = pairs(jnp.swapaxes(leaf, 0, 1))
    top = pairs(top_field)

    slots = jnp.arange(32, dtype=jnp.int32)

    def slot_of(positions):
        return jnp.sum(jnp.where(node_map[None, :] == positions[:, None], slots[None, :], 0), axis=1)

    mates = z * 4 + (j + jnp.arange(4)) % 4
    mate_pos = node_map[mates]
    left, right = slot_of(2 * mate_pos + 1), slot_of(2 * mate_pos + 2)
    plane = jnp.stack([left // 4, right // 4], axis=1).reshape(8)
    is_leaf = mate_pos[0] >= 15
    own = jnp.stack([jnp.where(is_leaf, 4, left[0] % 4), jnp.where(is_leaf, 4, right[0] % 4)])
    ring = ((z + jnp.arange(8)) % 8) * 4 + j
    ring_pos = node_map[ring]
    parent = slot_of((ring_pos - 1) // 2)
    pick = (parent % 4) * 2 + (1 - ring_pos % 2)
    from_z = jnp.where(ring_pos[:1] == 0, 8, parent[:1] // 4)
    tbl = jnp.concatenate([plane, own, pick, from_z]).astype(jnp.int32)

    vmem = pl.BlockSpec(memory_space=pltpu.VMEM)
    height = 64 // n_term
    dma = pltpu.SemaphoreType.DMA
    scratch = [
        pltpu.VMEM((256, 64), BF16),
        pltpu.VMEM((256, 64), BF16),
        pltpu.VMEM((2, 128, 256), BF16),
        pltpu.VMEM((2, 128, 256), BF16),
        pltpu.VMEM((256, 256), F32),
        pltpu.VMEM((256, 256), F32),
        pltpu.VMEM((256, 256), F32),
        pltpu.VMEM((256, 256), BF16),
        pltpu.VMEM((4, 256, 1024), BF16),
        pltpu.VMEM((4, 256, 1024), BF16),
        pltpu.VMEM((4, 256, 1024), BF16),
        pltpu.VMEM((4, 256, 1024), BF16),
        pltpu.VMEM((4, 256, 1024), BF16),
        pltpu.VMEM((4, 256, 1024), BF16),
        pltpu.VMEM((4, 256, 256), BF16),
        pltpu.VMEM((2, 128, 128), BF16),
        pltpu.VMEM((128, 128), BF16),
        pltpu.VMEM((n_term, height, 4096), BF16),
        pltpu.VMEM((n_term, height, 4096), BF16),
    ]
    scratch += [pltpu.VMEM((8, 128, 128), BF16)] * 4
    scratch += [pltpu.VMEM((4, 2, 128, 128), BF16)] * 4
    scratch += [pltpu.VMEM((5, 2, 128, 128), BF16)] * 4
    scratch += [pltpu.VMEM((8, 128, 128), BF16)] * 4
    scratch += [pltpu.VMEM((8, 128, 128), BF16)] * 4
    scratch += [pltpu.VMEM((9, 128, 128), BF16)] * 4
    scratch += [dma((32,)), dma((32,)), dma((16,)), dma((16,)), dma((16,)), dma((16,)), dma((32,)), dma((32,)), dma((8,)), dma((8,))]
    result = pl.pallas_call(
        functools.partial(kernel, n_term),
        out_shape=jax.ShapeDtypeStruct((height, 4096), BF16),
        in_specs=[pl.BlockSpec(memory_space=pltpu.SMEM)] + [vmem] * 7,
        out_specs=vmem,
        scratch_shapes=scratch,
        compiler_params=pltpu.CompilerParams(
            collective_id=0, has_side_effects=True, vmem_limit_bytes=60 * 1024 * 1024
        ),
    )(tbl, a1, a1p, a3, an2, an2p, leaf, top)
    return jnp.where(node_map[node] == 31, jnp.zeros_like(result), result)[None]


def solution(mesh):
    placed = (
        P("node", None, None),
        P("node", "term", None, None, None),
        P("node", "term", None),
        P("term", None, None),
        P(),
    )
    return jax.shard_map(
        functools.partial(per_device, mesh.shape["term"]),
        mesh=mesh,
        in_specs=placed,
        out_specs=P("node", "term", None),
        check_vma=False,
    )
```

time: 1190 us -> 191 us (0.16); the launches traced: 1180 us -> 191 us
  waiting for transfers between devices: 993 us -> 0 us
  Pallas kernels: 0 us -> 165 us
  local copies, waits for them, and re-layouts: 93.7 us -> 20.4 us
  matrix products: 50.1 us -> 0 us
  between operations: 24.2 us -> 1.29 us
    all_gather x8 -> x0, waiting for transfers between devices: 878 us -> none  [the longest x4 510 us: per_device(): gathered = lax.all_gather(both_sides[None], 'node', axis=0, tiled=True)]
    pallas_call x0 -> x1, Pallas kernels: none -> 165 us  [per_device(): pl.pallas_call(functools.partial(kernel, n_term), out_shape=jax.ShapeDtyp...]
    unnamed x10 -> x0, waiting for transfers between devices: 115 us -> none
    dot_general x36 -> x0, matrix products: 50.1 us -> none  [the longest x12 30.6 us: mode_one(): jnp.dot(matrix, tensor.reshape(extent, -1), preferred_element_type=jnp.fl...]
    convert_element_type x20 -> x0, local copies, waits for them, and re-layouts: 35.3 us -> none  [the longest x12 16.8 us: down_term(): reduced = mode_three(field_now, tensor).astype(jnp.bfloat16)]
    dot_general x12 -> x0, local copies, waits for them, and re-layouts: 13.3 us -> none  [mode_one(): jnp.dot(matrix, tensor.reshape(extent, -1), preferred_element_type=jnp.fl...]
  transfers between devices with their start and end apart: 9 -> 0, of which waited for: 9 -> 0; matrix products, arithmetic and copies ran while one was open for 0% -> 0% of each run, Pallas kernels for 0% -> 0%
where the time goes in v1:
time: 191 us
  Pallas kernels  165 us (86%)
  local copies, waits for them, and re-layouts  20.4 us (11%)
  other arithmetic  4.38 us (2%)
    pallas_call x1, Pallas kernels, per_device(): pl.pallas_call(functools.partial(kernel, n_term), out_shape=jax.ShapeDtyp...  165 us
    another operation x2, local copies, waits for them, and re-layouts, per_device(): tensor.reshape(64, 4, 4, 4, 64).transpose(2, 3, 4, 1, 0)  4.93 us

profile of v1, /device:TPU:24, one launch (start us, length us, event | category | flops | bytes accessed | tf_op | source)
XLA Modules:
  0.0 190.8 jit_solution(7636124360152276650)
XLA Ops:
  0.0 0.0 copy-start
  0.0 0.0 copy-start.1
  0.0 1.4 gather_fusion
  1.4 0.9 select_reduce_fusion.2
  2.3 0.1 copy.22
  2.4 0.1 reshape.278
  2.8 1.3 gather_fusion.1
  4.1 0.0 copy-done
  4.1 0.2 select_reduce_fusion
  4.5 0.6 concatenate.9.tbl
  5.1 0.0 copy-done.1
  5.1 1.1 reshape_reshape_squeeze.9
  6.3 0.7 copy.37
  6.9 1.5 reshape.279.a1
  8.5 1.1 reshape_squeeze.3
  9.6 0.7 copy.40
  10.3 0.7 copy.36
  11.0 1.5 reshape.281.a1p
  12.5 2.1 %reshape_reshape_squeeze.10 = bf16[64,4,4,4,64]{4,3,2,1,0:T(4,128)(2,1)} reshape(bf16[1,64,4096]{2,1,0:T(8,128)(2,1)S(1)} %copy-done.1) | data formatting | bytes 1048576 | tf_op jit(solution)/shard_map/reshape;reshape;squeeze | solution.py:361
  14.6 2.8 %copy.26 = bf16[64,4,4,4,64]{0,1,4,3,2:T(4,128)(2,1)S(1)} copy(bf16[64,4,4,4,64]{4,3,2,1,0:T(4,128)(2,1)} %reshape_reshape_squeeze.10) | data formatting | bytes 1048576 | tf_op jit(solution)/shard_map/reshape;reshape;squeeze | solution.py:361
  17.4 1.5 reshape.282.a3
  18.9 0.8 reshape.283
  19.7 0.0 copy-start.4
  19.7 0.0 copy-start.2
  19.8 0.0 copy-start.3
  19.8 1.6 pad_maximum_fusion
  21.4 0.0 copy-done.4
  21.4 0.1 copy.27
  21.5 0.0 copy-done.2
  21.6 0.1 bitcast_select_fusion
  21.6 0.1 copy.38
  21.8 0.7 reshape.285.leaf
  22.5 0.0 copy-done.3
  22.5 0.1 copy.39
  22.6 0.7 reshape.287.top
  23.3 164.8 %shard_map.55 = bf16[8,4096]{1,0:T(8,128)(2,1)} custom-call(s32[19]{0:T(128)} %concatenate.9.tbl, bf16[256,1024]{1,0:T(8,128)(2,1)} %reshape.279.a1, bf16[256,1024]{1,0:T(8,128)(2,1)} %reshape.281.a1p, bf16[4,256,256]{2,1,0:T(8,128)(2,1)} %reshape.282.a3, bf16[128,4096]{1,0:T(8,128)(2,1)} %get-tuple-element.13.an2, ...), custom_call_target="tpu_custom_call" | custom-call | tf_op jit(solution)/shard_map/pallas_call | solution.py:419
  188.1 0.6 dynamic_slice.3
  189.3 1.5 select_bitcast_fusion
  (11 shorter events, 0.1 us)
Async XLA Ops:
  0.0 4.1 %copy-start = (s32[32]{0:T(128)S(1)}, s32[32]{0:T(128)}, u32[]{:S(2)}) copy-start(s32[32]{0:T(128)} %param.9) | copy-start | bytes 388
  0.0 5.1 %copy-start.1 = (bf16[1,64,4096]{2,1,0:T(8,128)(2,1)S(1)}, bf16[1,64,4096]{2,1,0:T(8,128)(2,1)}, u32[]{:S(2)}) copy-start(bf16[1,64,4096]{2,1,0:T(8,128)(2,1)} %param.5) | copy-start | bytes 1572868
  19.7 1.7 copy-start.4
  19.7 1.8 copy-start.2
  19.8 2.8 %copy-start.3 = (bf16[4,64,64]{2,1,0:T(8,128)(2,1)S(1)}, bf16[4,64,64]{2,1,0:T(8,128)(2,1)}, u32[]{:S(2)}) copy-start(bf16[4,64,64]{2,1,0:T(8,128)(2,1)} %param.8) | copy-start | bytes 98308

commit v2 on v0

v2 whole, which is shorter than its diff:
```python
import functools

import jax
import jax.numpy as jnp
from jax import lax
from jax.experimental import pallas as pl
from jax.experimental.pallas import tpu as pltpu
from jax.sharding import PartitionSpec as P

MESH = pl.DeviceIdType.MESH
F32 = jnp.float32
BF16 = jnp.bfloat16
LEVELS = 4


def mm(x, y):
    return lax.dot_general(x, y, (((1,), (0,)), ((), ())), preferred_element_type=F32)


def mm_nt(x, y):
    return lax.dot_general(x, y, (((1,), (1,)), ((), ())), preferred_element_type=F32)


def iota(shape, dim):
    return lax.broadcasted_iota(jnp.int32, shape, dim)


def kernel(
    n_term,
    node_map,
    active,
    tensor,
    prim,
    top_field,
    out,
    nb,
    swb,
    a3,
    an2,
    an2p,
    e_r,
    e_l,
    j_r,
    j_l,
    m_r,
    m_l,
    m_m,
    perm,
    x_buf,
    y_buf,
    w_buf,
    ra_buf,
    la_buf,
    v_buf,
    bd_buf,
    lr_buf,
    m_buf,
    pieces,
    rs,
    *rest,
):
    zbuf, psend, prbuf, dpl, zsend, zr = (rest[8 * k : 8 * k + 8] for k in range(6))
    us, ur, ps, pr, ds_, dr, zs, zr_sem, ts, tr = rest[48:58]

    node = lax.axis_index("node")
    term = lax.axis_index("term")
    z = node // 4
    j = lax.rem(node, 4)

    def at_node(zt, jt):
        return {"node": zt * 4 + jt}

    partners = []
    for dz in range(1, 8):
        partners.append(at_node(lax.rem(z + dz, 8), j))
    for dj in range(1, 4):
        partners.append(at_node(z, lax.rem(j + dj, 4)))
    for dt in range(1, n_term):
        partners.append({"term": lax.rem(term + dt, n_term)})
    barrier = pltpu.get_barrier_semaphore()
    for partner in partners:
        pl.semaphore_signal(barrier, inc=1, device_id=partner, device_id_type=MESH)

    rows, cols = iota((256, 64), 0), iota((256, 64), 1)
    by, bx = rows // 16, lax.rem(rows // 4, 4)
    e_r[...] = jnp.where(cols == bx * 16 + by, 1.0, 0.0).astype(BF16)
    e_l[...] = jnp.where(cols == lax.rem(rows, 64), 1.0, 0.0).astype(BF16)
    rows, cols = iota((128, 256), 0), iota((128, 256), 1)
    for half in range(2):
        k = rows - 64 * half
        j_r[half] = jnp.where(k == lax.rem(cols, 64), 1.0, 0.0).astype(BF16)
        j_l[half] = jnp.where(k == lax.rem(cols, 4) * 16 + cols // 16, 1.0, 0.0).astype(BF16)
    rows, cols = iota((256, 256), 0), iota((256, 256), 1)
    m_r[...] = jnp.where(lax.rem(rows, 4) == cols // 64, 1.0, 0.0)
    same_bx = rows // 64 == lax.rem(cols // 4, 4)
    m_l[...] = jnp.where(same_bx, 1.0, 0.0)
    m_m[...] = jnp.where(rows // 64 == cols // 64, 1.0, 0.0)
    same_a = lax.rem(rows, 64) == lax.rem(cols, 4) * 16 + cols // 16
    perm[...] = jnp.where(same_bx & same_a, 1.0, 0.0).astype(BF16)
    same_lo = lax.rem(rows, 4) == cols // 64
    same_t = lax.rem(cols, 64) == lax.rem(rows // 4, 4) * 16 + rows // 16
    unit = jnp.where(same_lo & same_t, 1.0, 0.0).astype(BF16)
    eye = jnp.where(rows == cols, 1.0, 0.0).astype(BF16)
    eye64 = jnp.where(iota((64, 64), 0) == iota((64, 64), 1), 1.0, 0.0).astype(BF16)
    low = iota((16, 128), 1) < 64
    low64 = iota((64, 128), 1) < 64

    def expand(pair, half, e, jm, mask):
        spread = mm(e[...], pair).astype(BF16)
        return (mm(spread, jm[half]) * mask[...]).astype(BF16)

    def spread_mid(weight, src, dst, r):
        for g in range(4):
            o = mm(weight, src[:, g * 256 : (g + 1) * 256])
            for k in range(2):
                for i in range(8):
                    u = o[32 * i : 32 * i + 16, 128 * k : 128 * k + 128]
                    v = o[32 * i + 16 : 32 * i + 32, 128 * k : 128 * k + 128]
                    ur_, vr_ = pltpu.roll(u, 64, 1), pltpu.roll(v, 64, 1)
                    hi = (4 * g + 2 * k) * 16
                    lanes = slice(i * 128, i * 128 + 128)
                    dst[r, hi : hi + 16, lanes] = jnp.where(low, u, vr_).astype(BF16)
                    dst[r, hi + 16 : hi + 32, lanes] = jnp.where(low, ur_, v).astype(BF16)

    def op_on_mid(src, side, dst, hp):
        pair = lr_buf[hp, side]
        for half in range(2):
            spread_mid(expand(pair, half, e_r, j_r, m_r), src, dst, hp * 2 + half)

    def up(send, hp):
        op_on_mid(swb, 1, x_buf, hp)
        pair = lr_buf[hp, 0]
        both = []
        for half in range(2):
            weight = expand(pair, half, e_l, j_l, m_l)
            acc = jnp.zeros((256, 256), F32)
            for g in range(4):
                w = mm(weight, x_buf[hp * 2 + half, :, g * 256 : (g + 1) * 256]).astype(BF16)
                acc = acc + mm(a3[g], w)
            s = jnp.where(low64, acc[0:64, 0:128], acc[64:128, 0:128]) + jnp.where(
                low64, acc[128:192, 128:256], acc[192:256, 128:256]
            )
            both.append(s + pltpu.roll(s, 64, 1))
        send[z] = jnp.where(low64, both[0], both[1]).astype(BF16)

    def natural(src, dst, hp):
        for r in (2 * hp, 2 * hp + 1):
            for g in range(4):
                lanes = slice(g * 256, g * 256 + 256)
                dst[r, :, lanes] = mm(perm[...], src[r, :, lanes]).astype(BF16)

    def weighted(hp):
        for half in range(2):
            weight = expand(lr_buf[hp, 0], half, e_l, j_l, m_l)
            r = hp * 2 + half
            for g in range(4):
                lanes = slice(g * 256, g * 256 + 256)
                w_buf[r, :, lanes] = mm(weight, x_buf[r, :, lanes]).astype(BF16)

    def field(hp):
        for half in range(2):
            bd_buf[hp * 2 + half] = expand(m_buf[hp], half, e_l, j_r, m_m)

    def down(src, base, dst, slot, hp):
        for half in range(2):
            r = 2 * hp + half
            for g in range(4):
                lanes = slice(g * 256, g * 256 + 256)
                v = mm(src[r, :, lanes], bd_buf[r]).astype(BF16)
                for q in range(4):
                    v_buf[hp, q, half * 64 : half * 64 + 64, lanes] = v[q * 64 : q * 64 + 64]
        acc = jnp.zeros((128, 128), F32)
        for q in range(4):
            acc = acc + mm_nt(v_buf[hp, q], base[:, q * 1024 : q * 1024 + 1024])
        dst[slot] = jnp.where(low64, acc[0:64], acc[64:128]).astype(BF16)

    for q in range(4):
        nb[q * 64 : q * 64 + 64] = tensor[:, q * 1024 : q * 1024 + 1024]
    an2[0:64] = tensor[...]
    an2[64:128] = tensor[...]
    for g in range(4):
        a3[g] = mm_nt(eye, nb[:, g * 256 : g * 256 + 256]).astype(BF16)
    spread_mid(unit, nb, y_buf, 0)
    for g in range(4):
        lanes = slice(g * 256, g * 256 + 256)
        swb[:, lanes] = mm(perm[...], y_buf[0, :, lanes]).astype(BF16)
    for q in range(4):
        for dup in range(2):
            an2p[dup * 64 : dup * 64 + 64, q * 1024 : q * 1024 + 1024] = swb[q * 64 : q * 64 + 64]
    for hp in range(2):
        for side in range(2):
            ops = []
            for r in (2 * hp, 2 * hp + 1):
                acts = jnp.full((64, 64), active[r, side], jnp.int32) == 1
                ops.append(jnp.where(acts, prim[0, r, side], eye64))
            lr_buf[hp, side] = jnp.concatenate(ops, axis=1)
        m_buf[hp] = jnp.concatenate([top_field[2 * hp], top_field[2 * hp + 1]], axis=1)
        for level in range(LEVELS):
            prbuf[2 * level + hp][4] = lr_buf[hp]
            zr[2 * level + hp][8] = m_buf[hp]

    def own_slot(k):
        return z * 4 + lax.rem(j + k, 4)

    mates = [node_map[own_slot(k)] for k in range(4)]
    ring = [node_map[lax.rem(z + k, 8) * 4 + j] for k in range(8)]
    wanted = [2 * p + 1 for p in mates] + [2 * p + 2 for p in mates]

    def find(slot, found):
        here = node_map[slot]
        below = [jnp.where(here == want, slot, old) for want, old in zip(wanted, found[:8])]
        kids = (2 * here + 1, 2 * here + 2)
        above = [
            jnp.where((kids[0] == p) | (kids[1] == p), slot, old) for p, old in zip(ring, found[8:])
        ]
        return tuple(below + above)

    found = lax.fori_loop(0, 32, find, tuple(jnp.int32(0) for _ in range(16)))
    is_leaf = mates[0] >= 15
    tbl = []
    for k in range(4):
        tbl += [found[k] // 4, found[4 + k] // 4]
    tbl += [jnp.where(is_leaf, 4, lax.rem(found[side], 4)) for side in (0, 4)]
    tbl += [lax.rem(up_slot, 4) * 2 + 1 - lax.rem(p, 2) for up_slot, p in zip(found[8:], ring)]
    tbl.append(jnp.where(mates[0] == 0, 8, found[8] // 4))

    pending = []
    flight = {}

    def send(key, sems, slot, src, dst, to):
        copy = pltpu.make_async_remote_copy(
            src_ref=src,
            dst_ref=dst,
            send_sem=sems[0].at[slot],
            recv_sem=sems[1].at[slot],
            device_id=to,
            device_id_type=MESH,
        )
        copy.start()
        flight.setdefault(key, []).append(copy)
        pending.append(copy)

    def arrived(key):
        for copy in flight.pop(key):
            copy.wait_recv()

    def to_ring(dz):
        return at_node(lax.rem(z + dz, 8), j)

    def to_mate(dj):
        return at_node(z, lax.rem(j + dj, 4))

    def up_start(n):
        zb = zbuf[n]
        for dz in (4, 3, 5, 2, 6, 1, 7):
            send(("uz", n), (us, ur), n * 8 + dz, zb.at[z], zb.at[z], to_ring(dz))

    def up_relay(n):
        zb, sb, rb = zbuf[n], psend[n], prbuf[n]
        arrived(("uz", n))
        for dj in (2, 3, 1):
            sb[dj, 0] = zb[tbl[2 * dj]]
            sb[dj, 1] = zb[tbl[2 * dj + 1]]
            send(("up", n), (ps, pr), n * 4 + dj, sb.at[dj], rb.at[j], to_mate(dj))
        rb[j, 0] = zb[tbl[0]]
        rb[j, 1] = zb[tbl[1]]

    def up_finish(n):
        arrived(("up", n))
        lr_buf[n % 2, 0] = prbuf[n][tbl[8], 0]
        lr_buf[n % 2, 1] = prbuf[n][tbl[9], 1]

    for level in range(LEVELS):
        for hp in range(2):
            n = 2 * level + hp
            if level > 0:
                up_finish(n - 2)
            up(zbuf[n], hp)
            if n == 0:
                pl.semaphore_wait(barrier, len(partners))
            up_start(n)
        up_relay(2 * level)
        up_relay(2 * level + 1)

    def down_start(n):
        db = dpl[n]
        own = db.at[pl.ds(2 * j, 2)]
        for dj in (2, 3, 1):
            send(("dp", n), (ds_, dr), n * 4 + dj, own, own, to_mate(dj))

    def down_relay(n):
        db, sb, rb = dpl[n], zsend[n], zr[n]
        arrived(("dp", n))
        for dz in (4, 3, 5, 2, 6, 1, 7):
            sb[dz] = db[tbl[10 + dz]]
            send(("dz", n), (zs, zr_sem), n * 8 + dz, sb.at[dz], rb.at[z], to_ring(dz))
        rb[z] = db[tbl[10]]

    def down_finish(n):
        arrived(("dz", n))
        m_buf[n % 2] = zr[n][tbl[18]]

    for level in range(LEVELS):
        for hp in range(2):
            n = 2 * level + hp
            if level > 0:
                down_finish(n - 2)
            else:
                up_finish(2 * LEVELS - 2 + hp)
                op_on_mid(swb, 1, x_buf, hp)
                natural(x_buf, ra_buf, hp)
                op_on_mid(nb, 0, y_buf, hp)
                natural(y_buf, la_buf, hp)
            field(hp)
            down(ra_buf, an2, dpl[n], 2 * j, hp)
            down(la_buf, an2p, dpl[n], 2 * j + 1, hp)
            down_start(n)
        down_relay(2 * level)
        down_relay(2 * level + 1)
        if level == 0:
            weighted(0)
            weighted(1)

    for hp in range(2):
        down_finish(2 * LEVELS - 2 + hp)
        field(hp)
    height = 64 // n_term

    def last(g, _):
        lanes = pl.ds(pl.multiple_of(g * 256, 256), 256)
        acc = jnp.zeros((256, 256), F32)
        for r in range(4):
            acc = acc + mm(w_buf[r, :, lanes], bd_buf[r])
        for q in range(4):
            span = pl.ds(pl.multiple_of(q * 1024 + g * 256, 256), 256)
            for t in range(n_term):
                first = q * 64 + t * height
                pieces[t, :, span] = acc[first : first + height].astype(BF16)
        return 0

    lax.fori_loop(0, 4, last, 0)
    for dt in range(1, n_term):
        target = lax.rem(term + dt, n_term)
        send("t", (ts, tr), dt, pieces.at[target], rs.at[dt], {"term": target})
    total = pieces[term].astype(F32)
    if n_term > 1:
        arrived("t")
    for dt in range(1, n_term):
        total = total + rs[dt].astype(F32)
    absent = jnp.full(total.shape, mates[0], jnp.int32) == 31
    out[...] = jnp.where(absent, 0.0, total).astype(BF16)
    for copy in pending:
        copy.wait_send()


def per_device(n_term, node_tensors, prim_ops, active, top_field, node_map):
    vmem = pl.BlockSpec(memory_space=pltpu.VMEM)
    height = 64 // n_term
    dma = pltpu.SemaphoreType.DMA
    scratch = [
        pltpu.VMEM((256, 1024), BF16),
        pltpu.VMEM((256, 1024), BF16),
        pltpu.VMEM((4, 256, 256), BF16),
        pltpu.VMEM((128, 4096), BF16),
        pltpu.VMEM((128, 4096), BF16),
        pltpu.VMEM((256, 64), BF16),
        pltpu.VMEM((256, 64), BF16),
        pltpu.VMEM((2, 128, 256), BF16),
        pltpu.VMEM((2, 128, 256), BF16),
        pltpu.VMEM((256, 256), F32),
        pltpu.VMEM((256, 256), F32),
        pltpu.VMEM((256, 256), F32),
        pltpu.VMEM((256, 256), BF16),
        pltpu.VMEM((4, 256, 1024), BF16),
        pltpu.VMEM((4, 256, 1024), BF16),
        pltpu.VMEM((4, 256, 1024), BF16),
        pltpu.VMEM((4, 256, 1024), BF16),
        pltpu.VMEM((4, 256, 1024), BF16),
        pltpu.VMEM((2, 4, 128, 1024), BF16),
        pltpu.VMEM((4, 256, 256), BF16),
        pltpu.VMEM((2, 2, 64, 128), BF16),
        pltpu.VMEM((2, 64, 128), BF16),
        pltpu.VMEM((n_term, height, 4096), BF16),
        pltpu.VMEM((n_term, height, 4096), BF16),
    ]
    for lead in ((8,), (4, 2), (5, 2), (8,), (8,), (9,)):
        scratch += [pltpu.VMEM(lead + (64, 128), BF16)] * (2 * LEVELS)
    scratch += [dma((count,)) for count in (64, 64, 32, 32, 32, 32, 64, 64, 8, 8)]
    result = pl.pallas_call(
        functools.partial(kernel, n_term),
        out_shape=jax.ShapeDtypeStruct((height, 4096), BF16),
        in_specs=[pl.BlockSpec(memory_space=pltpu.SMEM)] * 2 + [vmem] * 3,
        out_specs=vmem,
        scratch_shapes=scratch,
        compiler_params=pltpu.CompilerParams(
            collective_id=0, has_side_effects=True, vmem_limit_bytes=60 * 1024 * 1024
        ),
    )(node_map, active[0], node_tensors[0], prim_ops, top_field)
    return result[None]


def solution(mesh):
    placed = (
        P("node", None, None),
        P("node", "term", None, None, None),
        P("node", "term", None),
        P("term", None, None),
        P(),
    )
    return jax.shard_map(
        functools.partial(per_device, mesh.shape["term"]),
        mesh=mesh,
        in_specs=placed,
        out_specs=P("node", "term", None),
        check_vma=False,
    )
```

time: 1190 us -> 121 us (0.10); the launches traced: 1180 us -> 121 us
  waiting for transfers between devices: 993 us -> 0 us
  Pallas kernels: 0 us -> 118 us
  local copies, waits for them, and re-layouts: 93.7 us -> 2.81 us
  matrix products: 50.1 us -> 0 us
  between operations: 24.2 us -> 0.01 us
  other arithmetic: 13.1 us -> 0 us
    all_gather x8 -> x0, waiting for transfers between devices: 878 us -> none  [the longest x4 510 us: per_device(): gathered = lax.all_gather(both_sides[None], 'node', axis=0, tiled=True)]
    pallas_call x0 -> x1, Pallas kernels: none -> 118 us  [per_device(): pl.pallas_call(functools.partial(kernel, n_term), out_shape=jax.ShapeDtyp...]
    unnamed x10 -> x0, waiting for transfers between devices: 115 us -> none
    dot_general x36 -> x0, matrix products: 50.1 us -> none  [the longest x12 30.6 us: mode_one(): jnp.dot(matrix, tensor.reshape(extent, -1), preferred_element_type=jnp.fl...]
    convert_element_type x20 -> x0, local copies, waits for them, and re-layouts: 35.3 us -> none  [the longest x12 16.8 us: down_term(): reduced = mode_three(field_now, tensor).astype(jnp.bfloat16)]
    another operation x16 -> x0, local copies, waits for them, and re-layouts: 15.5 us -> none  [the longest x4 4.5 us: up_term(): tensor.reshape(-1, extent)]
    reshape x12 -> x0, local copies, waits for them, and re-layouts: 14.7 us -> none  [the longest x8 11.5 us: mode_one(): tensor.reshape(extent, -1)]
    dot_general x12 -> x0, local copies, waits for them, and re-layouts: 13.3 us -> none  [mode_one(): jnp.dot(matrix, tensor.reshape(extent, -1), preferred_element_type=jnp.fl...]
  transfers between devices with their start and end apart: 9 -> 0, of which waited for: 9 -> 0; matrix products, arithmetic and copies ran while one was open for 0% -> 0% of each run, Pallas kernels for 0% -> 0%
where the time goes in v2:
time: 121 us
  Pallas kernels  118 us (98%)
  local copies, waits for them, and re-layouts  2.81 us (2%)
    pallas_call x1, Pallas kernels, per_device(): pl.pallas_call(functools.partial(kernel, n_term), out_shape=jax.ShapeDtyp...  118 us

profile of v2, /device:TPU:24, one launch (start us, length us, event | category | flops | bytes accessed | tf_op | source)
XLA Modules:
  0.0 121.3 jit_solution(13587064028438112961)
XLA Ops:
  0.0 0.0 copy-start
  0.0 0.7 copy-done
  0.7 0.7 copy.6.active
  1.3 118.4 %shard_map.55 = bf16[8,4096]{1,0:T(8,128)(2,1)} custom-call(s32[32]{0:T(128)} %node_map.1, s32[4,2]{1,0:T(4,128)} %copy.6.active, bf16[64,4096]{1,0:T(8,128)(2,1)} %bitcast.3, bf16[1,4,2,64,64]{4,3,2,1,0:T(8,128)(2,1)} %prim.1, bf16[4,64,64]{2,1,0:T(8,128)(2,1)} %top_field.1), custom_call_target="tpu_custom_call" | custom-call | tf_op jit(solution)/shard_map/pallas_call | solution.py:389
  119.8 1.5 %copy.8 = bf16[1,8,4096]{2,1,0:T(8,128)(2,1)} copy(bf16[1,8,4096]{2,1,0:T(8,128)(2,1)} %bitcast.4) | data formatting | bytes 131072
Async XLA Ops:
  0.0 0.7 copy-start

commit v3 on v2

v3 whole, which is shorter than its diff:
```python
import functools

import jax
import jax.numpy as jnp
from jax import lax
from jax.experimental import pallas as pl
from jax.experimental.pallas import tpu as pltpu
from jax.sharding import PartitionSpec as P

MESH = pl.DeviceIdType.MESH
F32 = jnp.float32
BF16 = jnp.bfloat16
LEVELS = 4


def mm(x, y):
    return lax.dot_general(x, y, (((1,), (0,)), ((), ())), preferred_element_type=F32)


def mm_nt(x, y):
    return lax.dot_general(x, y, (((1,), (1,)), ((), ())), preferred_element_type=F32)


def iota(shape, dim):
    return lax.broadcasted_iota(jnp.int32, shape, dim)


def kernel(
    n_term,
    node_map,
    inverse,
    active,
    tensor,
    prim,
    top_field,
    out,
    nb,
    swb,
    a3,
    e_r,
    e_l,
    j_r,
    j_l,
    m_r,
    m_l,
    m_m,
    perm,
    unit,
    x_buf,
    y_buf,
    w_buf,
    v_buf,
    bd_buf,
    lr_buf,
    sib_buf,
    m_buf,
    blk,
    sa_buf,
    za,
    pa_send,
    pa,
    ta_send,
    ta,
    pieces,
    rs,
    *rest,
):
    zbuf, psend, prbuf = (rest[8 * k : 8 * k + 8] for k in range(3))
    us, ur, ps, pr, azs, azr, aps, apr, ats, atr, ts, tr = rest[24:36]

    node = lax.axis_index("node")
    term = lax.axis_index("term")
    z = node // 4
    j = lax.rem(node, 4)

    def at_node(zt, jt):
        return {"node": zt * 4 + jt}

    partners = []
    for dz in range(1, 8):
        partners.append(at_node(lax.rem(z + dz, 8), j))
    for dj in range(1, 4):
        partners.append(at_node(z, lax.rem(j + dj, 4)))
    for dt in range(1, n_term):
        partners.append({"term": lax.rem(term + dt, n_term)})
    barrier = pltpu.get_barrier_semaphore()
    for partner in partners:
        pl.semaphore_signal(barrier, inc=1, device_id=partner, device_id_type=MESH)

    rows, cols = iota((256, 64), 0), iota((256, 64), 1)
    by, bx = rows // 16, lax.rem(rows // 4, 4)
    e_r[...] = jnp.where(cols == bx * 16 + by, 1.0, 0.0).astype(BF16)
    e_l[...] = jnp.where(cols == lax.rem(rows, 64), 1.0, 0.0).astype(BF16)
    rows, cols = iota((128, 256), 0), iota((128, 256), 1)
    for half in range(2):
        k = rows - 64 * half
        j_r[half] = jnp.where(k == lax.rem(cols, 64), 1.0, 0.0).astype(BF16)
        j_l[half] = jnp.where(k == lax.rem(cols, 4) * 16 + cols // 16, 1.0, 0.0).astype(BF16)
    rows, cols = iota((256, 256), 0), iota((256, 256), 1)
    m_r[...] = jnp.where(lax.rem(rows, 4) == cols // 64, 1.0, 0.0)
    same_bx = rows // 64 == lax.rem(cols // 4, 4)
    m_l[...] = jnp.where(same_bx, 1.0, 0.0)
    m_m[...] = jnp.where(rows // 64 == cols // 64, 1.0, 0.0)
    same_a = lax.rem(rows, 64) == lax.rem(cols, 4) * 16 + cols // 16
    perm[...] = jnp.where(same_bx & same_a, 1.0, 0.0).astype(BF16)
    same_lo = lax.rem(rows, 4) == cols // 64
    same_t = lax.rem(cols, 64) == lax.rem(rows // 4, 4) * 16 + rows // 16
    unit[...] = jnp.where(same_lo & same_t, 1.0, 0.0).astype(BF16)
    eye = jnp.where(rows == cols, 1.0, 0.0).astype(BF16)
    eye64 = jnp.where(iota((64, 64), 0) == iota((64, 64), 1), 1.0, 0.0).astype(BF16)
    low = iota((16, 128), 1) < 64
    low64 = iota((64, 128), 1) < 64

    def expand(pair, half, e, jm, mask):
        spread = mm(e[...], pair).astype(BF16)
        return (mm(spread, jm[half]) * mask[...]).astype(BF16)

    def spread_mid(weight, src, dst, r):
        for g in range(4):
            o = mm(weight, src(slice(g * 256, g * 256 + 256)))
            for k in range(2):
                for i in range(8):
                    u = o[32 * i : 32 * i + 16, 128 * k : 128 * k + 128]
                    v = o[32 * i + 16 : 32 * i + 32, 128 * k : 128 * k + 128]
                    ur_, vr_ = pltpu.roll(u, 64, 1), pltpu.roll(v, 64, 1)
                    hi = (4 * g + 2 * k) * 16
                    lanes = slice(i * 128, i * 128 + 128)
                    dst[r, hi : hi + 16, lanes] = jnp.where(low, u, vr_).astype(BF16)
                    dst[r, hi + 16 : hi + 32, lanes] = jnp.where(low, ur_, v).astype(BF16)

    def op_on_mid(src, side, dst, hp):
        pair = lr_buf[hp, side]
        for half in range(2):
            weight = expand(pair, half, e_r, j_r, m_r)
            spread_mid(weight, lambda lanes: src[:, lanes], dst, hp * 2 + half)

    def up(send, hp):
        op_on_mid(swb, 1, x_buf, hp)
        pair = lr_buf[hp, 0]
        both = []
        for half in range(2):
            weight = expand(pair, half, e_l, j_l, m_l)
            acc = jnp.zeros((256, 256), F32)
            for g in range(4):
                w = mm(weight, x_buf[hp * 2 + half, :, g * 256 : (g + 1) * 256]).astype(BF16)
                acc = acc + mm(a3[g], w)
            s = jnp.where(low64, acc[0:64, 0:128], acc[64:128, 0:128]) + jnp.where(
                low64, acc[128:192, 128:256], acc[192:256, 128:256]
            )
            both.append(s + pltpu.roll(s, 64, 1))
        send[z] = jnp.where(low64, both[0], both[1]).astype(BF16)

    def natural(src, r, dst):
        for g in range(4):
            lanes = slice(g * 256, g * 256 + 256)
            dst[:, lanes] = mm(perm[...], src[r, :, lanes]).astype(BF16)

    def weighted(hp):
        for half in range(2):
            weight = expand(lr_buf[hp, 0], half, e_l, j_l, m_l)
            r = hp * 2 + half
            for g in range(4):
                lanes = slice(g * 256, g * 256 + 256)
                w_buf[r, :, lanes] = mm(weight, x_buf[r, :, lanes]).astype(BF16)

    def field(k, hp):
        pair = m_buf[hp, k]
        for half in range(2):
            bd_buf[hp * 2 + half] = expand(pair, half, e_l, j_r, m_m)

    def walk(k, hp):
        field(k - 1, hp)
        for half in range(2):
            r = 2 * hp + half
            for g in range(4):
                lanes = slice(g * 256, g * 256 + 256)
                v = mm(sa_buf[k - 1, r, :, lanes], bd_buf[r]).astype(BF16)
                for q in range(4):
                    v_buf[hp, q, half * 64 : half * 64 + 64, lanes] = v[q * 64 : q * 64 + 64]
        acc = jnp.zeros((128, 64), F32)
        for q in range(4):
            acc = acc + mm_nt(v_buf[hp, q], blk[k - 1, base_of[k], q * 64 : q * 64 + 64, :])
        m_buf[hp, k] = jnp.concatenate([acc[0:64], acc[64:128]], axis=1).astype(BF16)

    def prepare(k, hp):
        for half in range(2):
            r = 2 * hp + half
            weight = expand(sib_buf[hp, k], half, e_r, j_r, m_r)
            spread_mid(weight, lambda lanes: blk[k - 1, 1 - base_of[k], :, lanes], y_buf, r)
            natural(y_buf, r, sa_buf.at[k - 1, r])

    for q in range(4):
        nb[q * 64 : q * 64 + 64] = tensor[:, q * 1024 : q * 1024 + 1024]
    for g in range(4):
        a3[g] = mm_nt(eye, nb[:, g * 256 : g * 256 + 256]).astype(BF16)
    y_unit = y_buf
    spread_mid(unit[...], lambda lanes: nb[:, lanes], y_unit, 0)
    natural(y_unit, 0, swb)
    for hp in range(2):
        for side in range(2):
            ops = []
            for r in (2 * hp, 2 * hp + 1):
                acts = jnp.full((64, 64), active[r, side], jnp.int32) == 1
                ops.append(jnp.where(acts, prim[0, r, side], eye64))
            lr_buf[hp, side] = jnp.concatenate(ops, axis=1)
        m_buf[hp, 0] = jnp.concatenate([top_field[2 * hp], top_field[2 * hp + 1]], axis=1)

    def slot_of(q):
        return inverse[jnp.maximum(jnp.minimum(q, 32) - 1, 0)]

    def at_depth(q, k):
        return (q >= 2**k) & (q < 2 ** (k + 1))

    def ancestor(q, k):
        best = jnp.int32(1)
        for up_by in range(6):
            best = jnp.where(at_depth(q // 2**up_by, k), q // 2**up_by, best)
        return best

    def sibling(q):
        return q + 1 - 2 * lax.rem(q, 2)

    here = [node_map[z * 4 + lax.rem(j + k, 4)] + 1 for k in range(4)]
    first_of, second_of, tensors_of = [], [], []
    for q in here:
        first_of.append(
            [
                slot_of(jnp.where(at_depth(q, k - 1), 2 * q, sibling(ancestor(q, k))))
                for k in range(1, 5)
            ]
        )
        second_of.append(slot_of(2 * q + 1))
        tensors_of.append([slot_of(ancestor(q, k)) for k in range(4)])
    base_of = [None] + [lax.rem(ancestor(here[0], k), 2) for k in range(1, 5)]
    depth = jnp.int32(0)
    for k in range(1, 5):
        depth = depth + jnp.where(here[0] >= 2**k, 1, 0)

    pending = []
    flight = {}

    def send(key, sems, slot, src, dst, to):
        copy = pltpu.make_async_remote_copy(
            src_ref=src,
            dst_ref=dst,
            send_sem=sems[0].at[slot],
            recv_sem=sems[1].at[slot],
            device_id=to,
            device_id_type=MESH,
        )
        copy.start()
        flight.setdefault(key, []).append(copy)
        pending.append(copy)

    def arrived(key):
        for copy in flight.pop(key):
            copy.wait_recv()

    def to_ring(dz):
        return at_node(lax.rem(z + dz, 8), j)

    def to_mate(dj):
        return at_node(z, lax.rem(j + dj, 4))

    def up_start(n):
        zb = zbuf[n]
        for dz in (4, 3, 5, 2, 6, 1, 7):
            send(("uz", n), (us, ur), n * 8 + dz, zb.at[z], zb.at[z], to_ring(dz))

    def up_relay(n):
        zb, sb, rb = zbuf[n], psend[n], prbuf[n]
        k = LEVELS - 1 - n // 2
        arrived(("uz", n))
        for dj in (2, 3, 1):
            sb[dj, 0] = zb[first_of[dj][k] // 4]
            sb[dj, 1] = zb[second_of[dj] // 4]
            send(("up", n), (ps, pr), n * 4 + dj, sb.at[dj], rb.at[j], to_mate(dj))
        rb[j, 0] = zb[first_of[0][k] // 4]
        rb[j, 1] = zb[second_of[0] // 4]

    def up_finish(n):
        k, hp = LEVELS - 1 - n // 2, n % 2
        rb = prbuf[n]
        rb[4] = lr_buf[hp]
        arrived(("up", n))
        mine = at_depth(here[0], k)
        first = lax.rem(first_of[0][k], 4)
        lr_buf[hp, 0] = rb[jnp.where(mine, first, 4), 0]
        lr_buf[hp, 1] = rb[jnp.where(mine, lax.rem(second_of[0], 4), 4), 1]
        sib_buf[hp, k + 1] = rb[first, 0]

    width = 4096 // n_term
    per_block = 1024 // width

    def fetch_start():
        mine = tensor.at[:, pl.ds(pl.multiple_of(term * width, width), width)]
        for dz in (4, 3, 5, 2, 6, 1, 7):
            send("az", (azs, azr), dz, mine, za.at[z], to_ring(dz))
        za[z] = tensor[:, pl.ds(pl.multiple_of(term * width, width), width)]

    def fetch_relay():
        arrived("az")
        for dj in (2, 3, 1):
            for k in range(4):
                pa_send[dj, k] = za[tensors_of[dj][k] // 4]
            send("ap", (aps, apr), dj, pa_send.at[dj], pa.at[j], to_mate(dj))
        for k in range(4):
            pa[j, k] = za[tensors_of[0][k] // 4]

    def fetch_share():
        arrived("ap")
        for k in range(4):
            ta_send[k] = pa[lax.rem(tensors_of[0][k], 4), k]
        send("ax", (ats, atr), 0, ta_send, ta.at[4], {"term": lax.rem(term + 4, 8)})

    row, column = term // 4, lax.rem(term, 4)

    def fetch_spread(part):
        cut = pl.ds(2 * part, 2)
        if part == 1:
            arrived("ax")
        for dy in (2, 1, 3):
            to = {"term": row * 4 + lax.rem(column + dy, 4)}
            slot = 8 * part + 8 + dy
            send(("at", part), (ats, atr), slot, ta_send.at[cut], ta.at[dy, cut], to)
            send(("at", part), (ats, atr), slot + 4, ta.at[4, cut], ta.at[4 + dy, cut], to)

    def fetch_finish(part):
        arrived(("at", part))
        for dt in range(8):
            source = lax.rem(row + dt // 4, 2) * 4 + lax.rem(column - dt % 4 + 4, 4)
            rows_at = pl.ds(pl.multiple_of((source // per_block) * 64, 64), 64)
            lanes_at = pl.ds(pl.multiple_of(lax.rem(source, per_block) * width, width), width)
            for k in (2 * part, 2 * part + 1):
                blk[k, 0, rows_at, lanes_at] = ta_send[k] if dt == 0 else ta[dt, k]

        def swap(k, _):
            spread_mid(unit[...], lambda lanes: blk[k, 0, :, lanes], y_buf, 0)
            natural(y_buf, 0, blk.at[k, 1])
            return 0

        lax.fori_loop(2 * part, 2 * part + 2, swap, 0)

    for level in range(LEVELS):
        for hp in range(2):
            n = 2 * level + hp
            if level > 0:
                up_finish(n - 2)
            up(zbuf[n], hp)
            if n == 0:
                pl.semaphore_wait(barrier, len(partners))
            up_start(n)
        if level == 0:
            fetch_start()
        if level == 2:
            fetch_spread(1)
        if level == 3:
            fetch_finish(1)
            for hp in range(2):
                prepare(4, hp)
        up_relay(2 * level)
        up_relay(2 * level + 1)
        if level == 0:
            fetch_relay()
        if level == 1:
            fetch_share()
        if level == 2:
            fetch_spread(0)
        if level == 3:
            for hp in range(2):
                prepare(3, hp)
            fetch_finish(0)
            for hp in range(2):
                prepare(2, hp)

    for hp in range(2):
        up_finish(2 * LEVELS - 2 + hp)
        prepare(1, hp)
        op_on_mid(swb, 1, x_buf, hp)
        weighted(hp)
    for k in range(1, 5):
        for hp in range(2):
            walk(k, hp)
    for hp in range(2):
        field(depth, hp)
    height = 64 // n_term

    def last(g, _):
        lanes = pl.ds(pl.multiple_of(g * 256, 256), 256)
        acc = jnp.zeros((256, 256), F32)
        for r in range(4):
            acc = acc + mm(w_buf[r, :, lanes], bd_buf[r])
        for q in range(4):
            span = pl.ds(pl.multiple_of(q * 1024 + g * 256, 256), 256)
            for t in range(n_term):
                first = q * 64 + t * height
                pieces[t, :, span] = acc[first : first + height].astype(BF16)
        return 0

    lax.fori_loop(0, 4, last, 0)
    for dt in range(1, n_term):
        target = lax.rem(term + dt, n_term)
        send("t", (ts, tr), dt, pieces.at[target], rs.at[dt], {"term": target})
    total = pieces[term].astype(F32)
    if n_term > 1:
        arrived("t")
    for dt in range(1, n_term):
        total = total + rs[dt].astype(F32)
    absent = jnp.full(total.shape, here[0], jnp.int32) == 32
    out[...] = jnp.where(absent, 0.0, total).astype(BF16)
    for copy in pending:
        copy.wait_send()


def per_device(n_term, node_tensors, prim_ops, active, top_field, node_map):
    vmem = pl.BlockSpec(memory_space=pltpu.VMEM)
    height = 64 // n_term
    dma = pltpu.SemaphoreType.DMA
    slots = jnp.arange(32, dtype=jnp.int32)
    inverse = jnp.sum(jnp.where(node_map[None, :] == slots[:, None], slots[None, :], 0), axis=1)
    width = 4096 // n_term
    scratch = [
        pltpu.VMEM((256, 1024), BF16),
        pltpu.VMEM((256, 1024), BF16),
        pltpu.VMEM((4, 256, 256), BF16),
        pltpu.VMEM((256, 64), BF16),
        pltpu.VMEM((256, 64), BF16),
        pltpu.VMEM((2, 128, 256), BF16),
        pltpu.VMEM((2, 128, 256), BF16),
        pltpu.VMEM((256, 256), F32),
        pltpu.VMEM((256, 256), F32),
        pltpu.VMEM((256, 256), F32),
        pltpu.VMEM((256, 256), BF16),
        pltpu.VMEM((256, 256), BF16),
        pltpu.VMEM((4, 256, 1024), BF16),
        pltpu.VMEM((4, 256, 1024), BF16),
        pltpu.VMEM((4, 256, 1024), BF16),
        pltpu.VMEM((2, 4, 128, 1024), BF16),
        pltpu.VMEM((4, 256, 256), BF16),
        pltpu.VMEM((2, 2, 64, 128), BF16),
        pltpu.VMEM((2, 5, 64, 128), BF16),
        pltpu.VMEM((2, 5, 64, 128), BF16),
        pltpu.VMEM((4, 2, 256, 1024), BF16),
        pltpu.VMEM((4, 4, 256, 1024), BF16),
        pltpu.VMEM((8, 64, width), BF16),
        pltpu.VMEM((4, 4, 64, width), BF16),
        pltpu.VMEM((4, 4, 64, width), BF16),
        pltpu.VMEM((4, 64, width), BF16),
        pltpu.VMEM((n_term, 4, 64, width), BF16),
        pltpu.VMEM((n_term, height, 4096), BF16),
        pltpu.VMEM((n_term, height, 4096), BF16),
    ]
    for lead in ((8,), (4, 2), (5, 2)):
        scratch += [pltpu.VMEM(lead + (64, 128), BF16)] * (2 * LEVELS)
    scratch += [dma((count,)) for count in (64, 64, 32, 32, 8, 8, 4, 4, 24, 24, 8, 8)]
    result = pl.pallas_call(
        functools.partial(kernel, n_term),
        out_shape=jax.ShapeDtypeStruct((height, 4096), BF16),
        in_specs=[pl.BlockSpec(memory_space=pltpu.SMEM)] * 3 + [vmem] * 3,
        out_specs=vmem,
        scratch_shapes=scratch,
        compiler_params=pltpu.CompilerParams(
            collective_id=0, has_side_effects=True, vmem_limit_bytes=60 * 1024 * 1024
        ),
    )(node_map, inverse, active[0], node_tensors[0], prim_ops, top_field)
    return result[None]


def solution(mesh):
    placed = (
        P("node", None, None),
        P("node", "term", None, None, None),
        P("node", "term", None),
        P("term", None, None),
        P(),
    )
    return jax.shard_map(
        functools.partial(per_device, mesh.shape["term"]),
        mesh=mesh,
        in_specs=placed,
        out_specs=P("node", "term", None),
        check_vma=False,
    )
```

time: 121 us -> 112 us (0.926)
  Pallas kernels: 118 us -> 108 us
    pallas_call x1, Pallas kernels: 118 us -> 108 us  [per_device(): pl.pallas_call(functools.partial(kernel, n_term), out_shape=jax.ShapeDtyp...]
where the time goes in v3:
time: 112 us; the launch traced here: 111 us
  Pallas kernels  108 us (96%)
  local copies, waits for them, and re-layouts  2.81 us (3%)
    pallas_call x1, Pallas kernels, per_device(): pl.pallas_call(functools.partial(kernel, n_term), out_shape=jax.ShapeDtyp...  108 us

profile of v3, /device:TPU:24, one launch (start us, length us, event | category | flops | bytes accessed | tf_op | source)
XLA Modules:
  0.0 111.3 jit_solution(3573738317739567196)
XLA Ops:
  0.0 0.0 copy-start.1
  0.0 0.7 copy-done.1
  0.7 0.0 copy-start
  0.7 0.7 select_reduce_fusion.inverse
  1.3 0.0 copy-done
  1.3 0.7 copy.7.active
  2.0 107.9 %shard_map.55 = bf16[8,4096]{1,0:T(8,128)(2,1)} custom-call(s32[32]{0:T(128)} %node_map.1, s32[32]{0:T(128)} %select_reduce_fusion.inverse, s32[4,2]{1,0:T(4,128)} %copy.7.active, bf16[64,4096]{1,0:T(8,128)(2,1)} %bitcast.3, bf16[1,4,2,64,64]{4,3,2,1,0:T(8,128)(2,1)} %prim.1, bf16[4,64,64]{2,1,0:T(8,128)(2,1)} %top_field.1), custom_call_target="tpu_custom_call" | custom-call | tf_op jit(solution)/shard_map/pallas_call | solution.py:456
  109.9 1.5 %copy.9 = bf16[1,8,4096]{2,1,0:T(8,128)(2,1)} copy(bf16[1,8,4096]{2,1,0:T(8,128)(2,1)} %bitcast.4) | data formatting | bytes 131072
Async XLA Ops:
  0.0 0.7 copy-start.1
  0.7 0.7 copy-start

commit v4 on v3

--- a/solution.py
+++ b/solution.py
@@ -312,18 +312,21 @@
         for k in range(4):
             ta_send[k] = pa[lax.rem(tensors_of[0][k], 4), k]
         send("ax", (ats, atr), 0, ta_send, ta.at[4], {"term": lax.rem(term + 4, 8)})
+        fetch_along(0, ta_send)
 
     row, column = term // 4, lax.rem(term, 4)
 
-    def fetch_spread(part):
-        cut = pl.ds(2 * part, 2)
-        if part == 1:
-            arrived("ax")
-        for dy in (2, 1, 3):
-            to = {"term": row * 4 + lax.rem(column + dy, 4)}
-            slot = 8 * part + 8 + dy
-            send(("at", part), (ats, atr), slot, ta_send.at[cut], ta.at[dy, cut], to)
-            send(("at", part), (ats, atr), slot + 4, ta.at[4, cut], ta.at[4 + dy, cut], to)
+    def fetch_along(first, source):
+        for part in (1, 0):
+            cut = pl.ds(2 * part, 2)
+            for dy in (2, 1, 3):
+                to = {"term": row * 4 + lax.rem(column + dy, 4)}
+                slot = 8 * part + 8 + first + dy
+                send(("at", part), (ats, atr), slot, source.at[cut], ta.at[first + dy, cut], to)
+
+    def fetch_spread():
+        arrived("ax")
+        fetch_along(4, ta.at[4])
 
     def fetch_finish(part):
         arrived(("at", part))
@@ -347,13 +350,15 @@
             if level > 0:
                 up_finish(n - 2)
             up(zbuf[n], hp)
-            if n == 0:
-                pl.semaphore_wait(barrier, len(partners))
-            up_start(n)
+            if level > 0:
+                up_start(n)
         if level == 0:
+            pl.semaphore_wait(barrier, len(partners))
+            up_start(0)
+            up_start(1)
             fetch_start()
         if level == 2:
-            fetch_spread(1)
+            fetch_spread()
         if level == 3:
             fetch_finish(1)
             for hp in range(2):
@@ -364,8 +369,6 @@
             fetch_relay()
         if level == 1:
             fetch_share()
-        if level == 2:
-            fetch_spread(0)
         if level == 3:
             for hp in range(2):
                 prepare(3, hp)

time: 112 us -> 108 us (0.964)
  Pallas kernels: 108 us -> 104 us
    pallas_call x1, Pallas kernels: 108 us -> 104 us  [per_device(): pl.pallas_call(functools.partial(kernel, n_term), out_shape=jax.ShapeDtyp...]
where the time goes in v4:
time: 108 us
  Pallas kernels  104 us (96%)
  local copies, waits for them, and re-layouts  2.81 us (3%)
    pallas_call x1, Pallas kernels, per_device(): pl.pallas_call(functools.partial(kernel, n_term), out_shape=jax.ShapeDtyp...  104 us

profile of v4, /device:TPU:24, one launch (start us, length us, event | category | flops | bytes accessed | tf_op | source)
XLA Modules:
  0.0 107.9 jit_solution(8382672127348040258)
XLA Ops:
  0.0 0.0 copy-start.1
  0.0 0.7 copy-done.1
  0.7 0.0 copy-start
  0.7 0.7 select_reduce_fusion.inverse
  1.3 0.0 copy-done
  1.3 0.7 copy.7.active
  2.0 104.4 %shard_map.55 = bf16[8,4096]{1,0:T(8,128)(2,1)} custom-call(s32[32]{0:T(128)} %node_map.1, s32[32]{0:T(128)} %select_reduce_fusion.inverse, s32[4,2]{1,0:T(4,128)} %copy.7.active, bf16[64,4096]{1,0:T(8,128)(2,1)} %bitcast.3, bf16[1,4,2,64,64]{4,3,2,1,0:T(8,128)(2,1)} %prim.1, bf16[4,64,64]{2,1,0:T(8,128)(2,1)} %top_field.1), custom_call_target="tpu_custom_call" | custom-call | tf_op jit(solution)/shard_map/pallas_call | solution.py:459
  106.4 1.5 %copy.9 = bf16[1,8,4096]{2,1,0:T(8,128)(2,1)} copy(bf16[1,8,4096]{2,1,0:T(8,128)(2,1)} %bitcast.4) | data formatting | bytes 131072
Async XLA Ops:
  0.0 0.7 copy-start.1
  0.7 0.7 copy-start

commit v5 on v4

--- a/solution.py
+++ b/solution.py
@@ -364,26 +364,34 @@
             for hp in range(2):
                 prepare(4, hp)
         up_relay(2 * level)
+        if level == 3:
+            prepare(3, 0)
         up_relay(2 * level + 1)
         if level == 0:
             fetch_relay()
         if level == 1:
             fetch_share()
         if level == 3:
-            for hp in range(2):
-                prepare(3, hp)
+            prepare(3, 1)
             fetch_finish(0)
-            for hp in range(2):
-                prepare(2, hp)
+
+    def own_weighted(hp):
+        op_on_mid(swb, 1, x_buf, hp)
+        weighted(hp)
 
     for hp in range(2):
         up_finish(2 * LEVELS - 2 + hp)
         prepare(1, hp)
-        op_on_mid(swb, 1, x_buf, hp)
-        weighted(hp)
-    for k in range(1, 5):
-        for hp in range(2):
-            walk(k, hp)
+        walk(1, hp)
+        prepare(2, hp)
+    walk(2, 0)
+    own_weighted(0)
+    walk(2, 1)
+    walk(3, 0)
+    own_weighted(1)
+    walk(3, 1)
+    walk(4, 0)
+    walk(4, 1)
     for hp in range(2):
         field(depth, hp)
     height = 64 // n_term

time: 108 us -> 108 us (level)
  no operation moved by 1% of the time
where the time goes in v5:
time: 108 us; the launch traced here: 107 us
  Pallas kernels  104 us (96%)
  local copies, waits for them, and re-layouts  2.81 us (3%)
    pallas_call x1, Pallas kernels, per_device(): pl.pallas_call(functools.partial(kernel, n_term), out_shape=jax.ShapeDtyp...  104 us

profile of v5, /device:TPU:24, one launch (start us, length us, event | category | flops | bytes accessed | tf_op | source)
XLA Modules:
  0.0 107.1 jit_solution(9469659887436837460)
XLA Ops:
  0.0 0.0 copy-start.1
  0.0 0.7 copy-done.1
  0.7 0.0 copy-start
  0.7 0.7 select_reduce_fusion.inverse
  1.3 0.0 copy-done
  1.3 0.7 copy.7.active
  2.0 103.6 %shard_map.55 = bf16[8,4096]{1,0:T(8,128)(2,1)} custom-call(s32[32]{0:T(128)} %node_map.1, s32[32]{0:T(128)} %select_reduce_fusion.inverse, s32[4,2]{1,0:T(4,128)} %copy.7.active, bf16[64,4096]{1,0:T(8,128)(2,1)} %bitcast.3, bf16[1,4,2,64,64]{4,3,2,1,0:T(8,128)(2,1)} %prim.1, bf16[4,64,64]{2,1,0:T(8,128)(2,1)} %top_field.1), custom_call_target="tpu_custom_call" | custom-call | tf_op jit(solution)/shard_map/pallas_call | solution.py:467
  105.6 1.5 %copy.9 = bf16[1,8,4096]{2,1,0:T(8,128)(2,1)} copy(bf16[1,8,4096]{2,1,0:T(8,128)(2,1)} %bitcast.4) | data formatting | bytes 131072
Async XLA Ops:
  0.0 0.7 copy-start.1
  0.7 0.7 copy-start
